TPU v7x, 512 devices: a whole 4x4x16 slice. The times are simulated.
512 devices in a mesh: row: 32 (over z, core), col: 16 (over y, x).
Axes of the slice: x: 4, y: 4, z: 16, core: 2. Of those that a mesh axis runs over, the one named last changes fastest.
Arguments:
- train_points: float32 [64, 32768], P(None, ('row', 'col')), may hold values from -6 to 6
- cand_points: float32 [64, 32768], P(None, ('row', 'col')), may hold values from -6 to 6
- inv_length: float32 [64], replicated, may hold values from 0.04 to 0.7
- noise: float32 [32768], P(('row', 'col')), may hold values from 0.5 to 4
- targets: float32 [16, 32768], P(None, ('row', 'col')), may hold values from -15 to 15
Outputs:
- solution: float32 [16, 32768], P(None, ('row', 'col'))
- post_mean: float32 [16, 32768], P(None, ('row', 'col'))
All inputs are finite; a program needn't handle non-finite values.
Results may differ from a plain program's by a relative error of at most 0.0047.
Values may be sent and summed in bfloat16 or wider, within the bound.
No kernel may reach another device: no remote copies, remote signals or barrier semaphores. Data moves between devices by JAX's collectives and lax.ppermute only.
A program may use at most 64 MiB of HBM per device.

v0:
```python
import math
import jax
import jax.numpy as jnp
from jax import lax
from jax.sharding import PartitionSpec as P

ITERS = 2
root_five = math.sqrt(5.0)


def matern(left, left_norm, right, right_norm):
    inner = lax.dot_general(
        left, right, (((0,), (0,)), ((), ())), preferred_element_type=jnp.float32
    )
    dist_sq = jnp.maximum(left_norm[:, None] + right_norm[None, :] - 2.0 * inner, 0.0)
    radius = jnp.sqrt(dist_sq)
    return (1.0 + root_five * radius + 5.0 / 3.0 * dist_sq) * jnp.exp(-root_five * radius)


def tile_rows(amount):
    best = 1
    for candidate in range(1, 513):
        if amount % candidate == 0:
            best = candidate
    return best


def accumulate(carried, vector_piece, piece_points, piece_norms, other, other_norms):
    amount = vector_piece.shape[1]
    block = tile_rows(amount)

    def advance(block_index, running):
        offset = block_index * block
        sub_points = lax.dynamic_slice_in_dim(piece_points, offset, block, 1)
        sub_norms = lax.dynamic_slice_in_dim(piece_norms, offset, block, 0)
        sub_vector = lax.dynamic_slice_in_dim(vector_piece, offset, block, 1)
        kernel_tile = matern(sub_points, sub_norms, other, other_norms)
        return running + jnp.dot(
            sub_vector,
            kernel_tile,
            precision=lax.Precision.HIGHEST,
            preferred_element_type=jnp.float32,
        )

    return lax.fori_loop(0, amount // block, advance, carried)


def per_device(train_points, cand_points, inv_length, noise, targets):
    scaled_train = (train_points * inv_length[:, None]).astype(jnp.bfloat16)
    scaled_cand = (cand_points * inv_length[:, None]).astype(jnp.bfloat16)
    row_train, row_cand = (
        lax.all_gather(scaled_train, "col", axis=1, tiled=True),
        lax.all_gather(scaled_cand, "col", axis=1, tiled=True),
    )
    col_train = lax.all_gather(scaled_train, "row", axis=1, tiled=True)
    row_norms = jnp.sum(jnp.square(row_train.astype(jnp.float32)), axis=0)
    cand_norms = jnp.sum(jnp.square(row_cand.astype(jnp.float32)), axis=0)
    col_norms = jnp.sum(jnp.square(col_train.astype(jnp.float32)), axis=0)
    outputs = targets.shape[0]

    def from_columns(other, other_norms, carried, vector_piece):
        return accumulate(carried, vector_piece, col_train, col_norms, other, other_norms)

    def squares(residual):
        return lax.psum(jnp.sum(residual * residual, axis=1), ("row", "col"))

    solution = jnp.zeros_like(targets)
    residual = targets
    direction = targets
    norm_now = squares(residual)
    for iteration in range(ITERS):
        start_total = jnp.zeros((outputs, row_train.shape[1]), jnp.float32)
        partial_image = from_columns(
            row_train, row_norms, start_total, lax.all_gather(direction, "row", axis=1, tiled=True)
        )
        own_image = lax.psum_scatter(partial_image, "col", scatter_dimension=1, tiled=True)
        image = own_image + noise[None, :] * direction
        alpha = norm_now / lax.psum(jnp.sum(direction * image, axis=1), ("row", "col"))
        solution = solution + alpha[:, None] * direction
        residual = residual - alpha[:, None] * image
        norm_next = squares(residual)
        direction = residual + (norm_next / norm_now)[:, None] * direction
        norm_now = norm_next
    mean_start = jnp.zeros((outputs, row_cand.shape[1]), jnp.float32)
    partial_mean = from_columns(
        row_cand, cand_norms, mean_start, lax.all_gather(solution, "row", axis=1, tiled=True)
    )
    post_mean = lax.psum_scatter(partial_mean, "col", scatter_dimension=1, tiled=True)
    return (solution, post_mean)


def solution(mesh):
    placed = (
        P(None, ("row", "col")),
        P(None, ("row", "col")),
        P(),
        P(("row", "col")),
        P(None, ("row", "col")),
    )
    return jax.shard_map(
        per_device,
        mesh=mesh,
        in_specs=placed,
        out_specs=(P(None, ("row", "col")), P(None, ("row", "col"))),
        check_vma=False,
    )
```

profile of v0, /device:TPU:2, one launch (start us, length us, event | category | flops | bytes accessed | tf_op | source)
XLA Modules:
  0.0 763.7 jit_solution(8951887657408759057)
XLA Ops:
  7.2 0.8 copy.22
  8.1 0.8 copy.29
  8.9 0.7 multiply_convert_fusion
  9.6 37.6 %all_gather.19 = bf16[64,2048]{0,1:T(8,128)(2,1)S(1)} all-gather(bf16[64,64]{0,1:T(8,128)(2,1)S(1)} %get-tuple-element.538), channel_id=1, replica_groups=mesh['row'=32,'col'=16] {'row'}, dimensions={1}, use_global_device_ids=true | all-gather | bytes 270336 | tf_op jit(solution)/shard_map/all_gather | solution.py:55
  47.8 23.8 %all_gather.20 = bf16[64,1024]{0,1:T(8,128)(2,1)S(1)} all-gather(bf16[64,64]{0,1:T(8,128)(2,1)S(1)} %get-tuple-element.538), channel_id=1, replica_groups=mesh['row'=32,'col'=16] {'col'}, dimensions={1}, use_global_device_ids=true | all-gather | bytes 139264 | tf_op jit(solution)/shard_map/all_gather | solution.py:52
  71.9 27.5 %all-gather = f32[32,64,16]{1,2,0:T(8,128)S(1)} all-gather(f32[1,64,16]{1,2,0:T(8,128)S(1)} %bitcast.37), channel_id=1, replica_groups=mesh['row'=32,'col'=16] {'row'}, dimensions={0}, use_global_device_ids=true | all-gather | bytes 135168 | tf_op jit(solution)/shard_map/all_gather | solution.py:74
  99.6 11.9 %while.42 = (s32[]{:T(128)}, f32[16,1024]{1,0:T(8,128)S(1)}, f32[16,2048]{1,0:T(8,128)S(1)}, f32[2048]{0:T(1024)S(1)}, f32[1024]{0:T(1024)S(1)}, /*index=5*/bf16...) while((s32[]{:T(128)}, f32[16,1024]{1,0:T(8,128)S(1)}, ...), condition=%wide.region_5.0_spmd.clone, body=%wide.region_4.0_spmd.clone.sunk | while | flops 173047808 | bytes 4565169 | solution.py:45
  99.7 0.5 fusion.131
  100.2 2.4 fusion.132
  102.6 0.5 fusion.131
  103.2 2.4 fusion.132
  105.6 0.5 fusion.131
  106.1 2.4 fusion.132
  108.6 0.5 fusion.131
  109.1 2.4 fusion.132
  111.6 1.0 copy.32
  112.6 83.7 %reduce-scatter.10.cloned.1.call-done = f32[64,16]{1,0:T(8,128)} async-done(((f32[1024,16]{1,0:T(8,128)}), f32[64,16]{1,0:T(8,128)}) %reduce-scatter.10.cloned.1.call-update) | async-done | bytes 4112
  196.4 0.8 copy.33
  197.3 101.8 %all-reduce = (f32[16]{0:T(128)S(1)}, f32[16]{0:T(128)S(1)}) all-reduce(f32[16]{0:T(128)S(1)} %get-tuple-element.492, f32[16]{0:T(128)S(1)} %get-tuple-element.491), channel_id=1, replica_groups=mesh['row'=32,'col'=16] {'row','col'}, use_global_device_ids=true, to_apply=%region_1.0 | all-reduce | flops 32 | bytes 256 | tf_op jit(solution)/shard_map/psum | solution.py:65
  299.3 100.8 %psum.30 = f32[16]{0:T(128)S(1)} all-reduce(f32[16]{0:T(128)S(1)} %multiply_reduce_fusion.4), channel_id=1, replica_groups=mesh['row'=32,'col'=16] {'row','col'}, use_global_device_ids=true, to_apply=%region_10.0 | all-reduce | flops 16 | bytes 128 | tf_op jit(solution)/shard_map/psum | solution.py:65
  400.3 28.5 %all-gather.1 = f32[32,64,16]{1,2,0:T(8,128)S(1)} all-gather(f32[1,64,16]{1,2,0:T(8,128)S(1)} %fusion.105), channel_id=1, replica_groups=mesh['row'=32,'col'=16] {'row'}, dimensions={0}, use_global_device_ids=true | all-gather | bytes 135168 | tf_op jit(solution)/shard_map/all_gather | solution.py:74
  429.0 11.9 %while.43 = (s32[]{:T(128)}, f32[16,1024]{1,0:T(8,128)S(1)}, f32[16,2048]{1,0:T(8,128)S(1)}, f32[2048]{0:T(1024)S(1)}, f32[1024]{0:T(1024)S(1)}, /*index=5*/bf16...) while((s32[]{:T(128)}, f32[16,1024]{1,0:T(8,128)S(1)}, ...), condition=%wide.region_12.0_spmd.clone, body=%wide.region_11.0_spmd.clone.sunk | while | flops 173047808 | bytes 4565169 | solution.py:45
  429.0 0.5 fusion.137
  429.5 2.4 fusion.138
  432.0 0.5 fusion.137
  432.5 2.4 fusion.138
  435.0 0.5 fusion.137
  435.5 2.4 fusion.138
  437.9 0.5 fusion.137
  438.5 2.4 fusion.138
  440.9 1.0 copy.34
  442.0 22.1 %all_gather.23 = bf16[64,1024]{0,1:T(8,128)(2,1)S(1)} all-gather(bf16[64,64]{0,1:T(8,128)(2,1)S(1)} %get-tuple-element.537), channel_id=1, replica_groups=mesh['row'=32,'col'=16] {'col'}, dimensions={1}, use_global_device_ids=true | all-gather | bytes 139264 | tf_op jit(solution)/shard_map/all_gather | solution.py:53
  464.4 60.8 %reduce-scatter.12.cloned.1.call-done = f32[64,16]{1,0:T(8,128)} async-done(((f32[1024,16]{1,0:T(8,128)}), f32[64,16]{1,0:T(8,128)}) %reduce-scatter.12.cloned.1.call-update) | async-done | bytes 4112
  525.2 0.8 copy.35
  526.2 102.1 %psum.31 = f32[16]{0:T(128)S(1)} all-reduce(f32[16]{0:T(128)S(1)} %multiply_reduce_fusion.3), channel_id=1, replica_groups=mesh['row'=32,'col'=16] {'row','col'}, use_global_device_ids=true, to_apply=%region_15.0 | all-reduce | flops 16 | bytes 128 | tf_op jit(solution)/shard_map/psum | solution.py:78
  628.4 28.8 %all-gather.2 = f32[32,64,16]{1,2,0:T(8,128)S(1)} all-gather(f32[1,64,16]{1,2,0:T(8,128)S(1)} %bitcast.44), channel_id=1, replica_groups=mesh['row'=32,'col'=16] {'row'}, dimensions={0}, use_global_device_ids=true | all-gather | bytes 135168 | tf_op jit(solution)/shard_map/all_gather | solution.py:86
  657.4 11.9 %while.44 = (s32[]{:T(128)}, f32[16,1024]{1,0:T(8,128)S(1)}, f32[16,2048]{1,0:T(8,128)S(1)}, f32[2048]{0:T(1024)S(1)}, f32[1024]{0:T(1024)S(1)}, /*index=5*/bf16...) while((s32[]{:T(128)}, f32[16,1024]{1,0:T(8,128)S(1)}, ...), condition=%wide.region_18.0_spmd.clone, body=%wide.region_17.0_spmd.clone.sunk | while | flops 173047808 | bytes 4565169 | solution.py:45
  657.4 0.5 fusion.143
  658.0 2.4 fusion.144
  660.4 0.5 fusion.143
  660.9 2.4 fusion.144
  663.4 0.5 fusion.143
  663.9 2.4 fusion.144
  666.3 0.5 fusion.143
  666.9 2.4 fusion.144
  669.3 1.0 copy.36
  670.3 85.4 %reduce-scatter.14.cloned.1.call-done = f32[64,16]{1,0:T(8,128)} async-done(((f32[1024,16]{1,0:T(8,128)}), f32[64,16]{1,0:T(8,128)}) %reduce-scatter.14.cloned.1.call-update) | async-done | bytes 4112
  755.7 1.4 copy.37
  (47 shorter events, 3.6 us)
Async XLA Ops:
  7.2 64.7 %copy-start = (f32[16,64]{1,0:T(8,128)S(1)}, f32[16,64]{1,0:T(8,128)}, u32[]{:S(2)}) copy-start(f32[16,64]{1,0:T(8,128)} %param.15) | copy-start | bytes 12292
  7.2 189.2 %reduce-scatter.10.cloned.1.call-start = ((), (), s32[]{:S(2)}) async-start(), calls=%async_computation.3 | async-start | bytes 557056
  99.6 97.6 %copy-start.2 = (f32[64]{0:T(128)S(1)}, f32[64]{0:T(128)}, u32[]{:S(2)}) copy-start(f32[64]{0:T(128)} %param.14) | copy-start | bytes 772
  112.6 412.6 %reduce-scatter.12.cloned.1.call-start = ((), (), s32[]{:S(2)}) async-start(), calls=%async_computation.4 | async-start | bytes 557056
  441.9 313.8 %reduce-scatter.14.cloned.1.call-start = ((), (), s32[]{:S(2)}) async-start(), calls=%async_computation.5 | async-start | bytes 557056
  628.4 29.0 %copy-start.1 = (f32[16,64]{1,0:T(8,128)}, f32[16,64]{1,0:T(8,128)S(1)}, u32[]{:S(2)}) copy-start(f32[16,64]{1,0:T(8,128)S(1)} %multiply_add_fusion) | copy-start | bytes 12292
Sparse Core Ops, SparseCore 0:
  112.7 83.6 reduce-scatter.9
  442.1 83.1 reduce-scatter.11
  670.5 85.2 reduce-scatter.13
where the time goes:
time: 764 us
  blocking collectives  473 us (62%)
  waiting for transfers between devices  230 us (30%)
  matrix products  34.7 us (5%)
  between operations  13.9 us (2%)
  local copies, waits for them, and re-layouts  9.77 us (1%)
    unnamed x6, waiting for transfers between devices  230 us
    psum x2, blocking collectives, squares(): return lax.psum(jnp.sum(residual * residual, axis=1), ('row', 'col'))  203 us
    psum x1, blocking collectives, per_device(): lax.psum(jnp.sum(direction * image, axis=1), ('row', 'col'))  102 us
    all_gather x2, blocking collectives, per_device(): lax.all_gather(direction, 'row', axis=1, tiled=True)  56 us
    all_gather x1, blocking collectives, per_device(): col_train = lax.all_gather(scaled_train, 'row', axis=1, tiled=True)  37.6 us
    dot_general x12, matrix products, advance(): jnp.dot(sub_vector, kernel_tile, precision=lax.Precision.HIGHEST, preferr...  29.1 us
    all_gather x1, blocking collectives, per_device(): lax.all_gather(solution, 'row', axis=1, tiled=True)  28.8 us
    all_gather x1, blocking collectives, per_device(): lax.all_gather(scaled_train, 'col', axis=1, tiled=True)  23.8 us
  transfers between devices with their start and end apart: 3, of which 3 were waited for; matrix products, arithmetic and copies ran while one was open for 0% of the time, Pallas kernels for 0%

commit v1 on v0

--- a/solution.py
+++ b/solution.py
@@ -6,6 +6,11 @@
 
 ITERS = 2
 root_five = math.sqrt(5.0)
+
+
+def by_each_axis(x, first, second):
+    half = lax.psum(x, first)
+    return lax.psum(half, second)
 
 
 def matern(left, left_norm, right, right_norm):
@@ -62,7 +67,7 @@
         return accumulate(carried, vector_piece, col_train, col_norms, other, other_norms)
 
     def squares(residual):
-        return lax.psum(jnp.sum(residual * residual, axis=1), ("row", "col"))
+        return by_each_axis(jnp.sum(residual * residual, axis=1), "col", "row")
 
     solution = jnp.zeros_like(targets)
     residual = targets

time: 764 us -> 829 us (1.085)
  blocking collectives: 473 us -> 536 us
    psum x1 -> x2, blocking collectives: 102 us -> 203 us  [per_device(): lax.psum(jnp.sum(direction * image, axis=1), ('row', 'col'))]
    psum x2 -> x4, blocking collectives: 203 us -> 166 us  [the longest x2 92.2 us: by_each_axis(): return lax.psum(half, second)]
where the time goes in v1:
time: 829 us; the launch traced here: 828 us
  blocking collectives  536 us (65%)
  waiting for transfers between devices  231 us (28%)
  matrix products  34.7 us (4%)
  between operations  13.9 us (2%)
  local copies, waits for them, and re-layouts  9.76 us (1%)
    unnamed x6, waiting for transfers between devices  231 us
    psum x2, blocking collectives, per_device(): lax.psum(jnp.sum(direction * image, axis=1), ('row', 'col'))  203 us
    psum x2, blocking collectives, by_each_axis(): return lax.psum(half, second)  92.2 us
    psum x2, blocking collectives, by_each_axis(): half = lax.psum(x, first)  73.8 us
    all_gather x2, blocking collectives, per_device(): lax.all_gather(direction, 'row', axis=1, tiled=True)  55.2 us
    all_gather x1, blocking collectives, per_device(): col_train = lax.all_gather(scaled_train, 'row', axis=1, tiled=True)  37.6 us
    dot_general x12, matrix products, advance(): jnp.dot(sub_vector, kernel_tile, precision=lax.Precision.HIGHEST, preferr...  29.1 us
    all_gather x1, blocking collectives, per_device(): lax.all_gather(solution, 'row', axis=1, tiled=True)  29 us
  transfers between devices with their start and end apart: 3, of which 3 were waited for; matrix products, arithmetic and copies ran while one was open for 0% of the time, Pallas kernels for 0%

profile of v1, /device:TPU:2, one launch (start us, length us, event | category | flops | bytes accessed | tf_op | source)
XLA Modules:
  0.0 828.1 jit_solution(1754194843599600129)
XLA Ops:
  7.2 0.8 copy.22
  8.1 0.8 copy.29
  8.9 0.7 multiply_convert_fusion
  9.6 37.6 %all_gather.19 = bf16[64,2048]{0,1:T(8,128)(2,1)S(1)} all-gather(bf16[64,64]{0,1:T(8,128)(2,1)S(1)} %get-tuple-element.536), channel_id=1, replica_groups=mesh['row'=32,'col'=16] {'row'}, dimensions={1}, use_global_device_ids=true | all-gather | bytes 270336 | tf_op jit(solution)/shard_map/all_gather | solution.py:60
  47.8 23.8 %all_gather.20 = bf16[64,1024]{0,1:T(8,128)(2,1)S(1)} all-gather(bf16[64,64]{0,1:T(8,128)(2,1)S(1)} %get-tuple-element.536), channel_id=1, replica_groups=mesh['row'=32,'col'=16] {'col'}, dimensions={1}, use_global_device_ids=true | all-gather | bytes 139264 | tf_op jit(solution)/shard_map/all_gather | solution.py:57
  71.9 27.5 %all-gather = f32[32,64,16]{1,2,0:T(8,128)S(1)} all-gather(f32[1,64,16]{1,2,0:T(8,128)S(1)} %bitcast.37), channel_id=1, replica_groups=mesh['row'=32,'col'=16] {'row'}, dimensions={0}, use_global_device_ids=true | all-gather | bytes 135168 | tf_op jit(solution)/shard_map/all_gather | solution.py:79
  99.6 11.9 %while.42 = (s32[]{:T(128)}, f32[16,1024]{1,0:T(8,128)S(1)}, f32[16,2048]{1,0:T(8,128)S(1)}, f32[2048]{0:T(1024)S(1)}, f32[1024]{0:T(1024)S(1)}, /*index=5*/bf16...) while((s32[]{:T(128)}, f32[16,1024]{1,0:T(8,128)S(1)}, ...), condition=%wide.region_6.0_spmd.clone, body=%wide.region_5.0_spmd.clone.sunk | while | flops 173047808 | bytes 4565169 | solution.py:50
  100.2 2.4 fusion.132
  102.6 0.5 fusion.131
  103.2 2.4 fusion.132
  105.6 0.5 fusion.131
  106.1 2.4 fusion.132
  108.6 0.5 fusion.131
  109.1 2.4 fusion.132
  111.6 1.0 copy.32
  112.6 83.7 %reduce-scatter.10.cloned.1.call-done = f32[64,16]{1,0:T(8,128)} async-done(((f32[1024,16]{1,0:T(8,128)}), f32[64,16]{1,0:T(8,128)}) %reduce-scatter.10.cloned.1.call-update) | async-done | bytes 4112
  196.4 0.8 copy.33
  197.3 36.3 %psum.42 = f32[16]{0:T(128)S(1)} all-reduce(f32[16]{0:T(128)S(1)} %get-tuple-element.492), channel_id=1, replica_groups=mesh['row'=32,'col'=16] {'col'}, use_global_device_ids=true, to_apply=%region_1.0 | all-reduce | flops 16 | bytes 128 | tf_op jit(solution)/shard_map/psum | solution.py:12
  233.6 46.5 %psum.43 = f32[16]{0:T(128)S(1)} all-reduce(f32[16]{0:T(128)S(1)} %psum.42), channel_id=1, replica_groups=mesh['row'=32,'col'=16] {'row'}, use_global_device_ids=true, to_apply=%region_2.0 | all-reduce | flops 16 | bytes 128 | tf_op jit(solution)/shard_map/psum | solution.py:13
  280.1 100.7 %psum.44 = f32[16]{0:T(128)S(1)} all-reduce(f32[16]{0:T(128)S(1)} %get-tuple-element.491), channel_id=1, replica_groups=mesh['row'=32,'col'=16] {'row','col'}, use_global_device_ids=true, to_apply=%region_9.0 | all-reduce | flops 16 | bytes 128 | tf_op jit(solution)/shard_map/psum | solution.py:83
  381.0 37.5 %psum.45 = f32[16]{0:T(128)S(1)} all-reduce(f32[16]{0:T(128)S(1)} %multiply_reduce_fusion.4), channel_id=1, replica_groups=mesh['row'=32,'col'=16] {'col'}, use_global_device_ids=true, to_apply=%region_11.0 | all-reduce | flops 16 | bytes 128 | tf_op jit(solution)/shard_map/psum | solution.py:12
  418.4 45.8 %psum.46 = f32[16]{0:T(128)S(1)} all-reduce(f32[16]{0:T(128)S(1)} %psum.45), channel_id=1, replica_groups=mesh['row'=32,'col'=16] {'row'}, use_global_device_ids=true, to_apply=%region_12.0 | all-reduce | flops 16 | bytes 128 | tf_op jit(solution)/shard_map/psum | solution.py:13
  464.3 27.7 %all-gather.1 = f32[32,64,16]{1,2,0:T(8,128)S(1)} all-gather(f32[1,64,16]{1,2,0:T(8,128)S(1)} %fusion.105), channel_id=1, replica_groups=mesh['row'=32,'col'=16] {'row'}, dimensions={0}, use_global_device_ids=true | all-gather | bytes 135168 | tf_op jit(solution)/shard_map/all_gather | solution.py:79
  492.2 11.9 %while.43 = (s32[]{:T(128)}, f32[16,1024]{1,0:T(8,128)S(1)}, f32[16,2048]{1,0:T(8,128)S(1)}, f32[2048]{0:T(1024)S(1)}, f32[1024]{0:T(1024)S(1)}, /*index=5*/bf16...) while((s32[]{:T(128)}, f32[16,1024]{1,0:T(8,128)S(1)}, ...), condition=%wide.region_14.0_spmd.clone, body=%wide.region_13.0_spmd.clone.sunk | while | flops 173047808 | bytes 4565169 | solution.py:50
  492.7 2.4 fusion.138
  495.2 0.5 fusion.137
  495.7 2.4 fusion.138
  498.1 0.5 fusion.137
  498.7 2.4 fusion.138
  501.1 0.5 fusion.137
  501.7 2.4 fusion.138
  504.1 1.0 copy.34
  505.2 22.2 %all_gather.23 = bf16[64,1024]{0,1:T(8,128)(2,1)S(1)} all-gather(bf16[64,64]{0,1:T(8,128)(2,1)S(1)} %get-tuple-element.535), channel_id=1, replica_groups=mesh['row'=32,'col'=16] {'col'}, dimensions={1}, use_global_device_ids=true | all-gather | bytes 139264 | tf_op jit(solution)/shard_map/all_gather | solution.py:58
  527.7 61.8 %reduce-scatter.12.cloned.1.call-done = f32[64,16]{1,0:T(8,128)} async-done(((f32[1024,16]{1,0:T(8,128)}), f32[64,16]{1,0:T(8,128)}) %reduce-scatter.12.cloned.1.call-update) | async-done | bytes 4112
  589.6 0.8 copy.35
  590.6 101.9 %psum.47 = f32[16]{0:T(128)S(1)} all-reduce(f32[16]{0:T(128)S(1)} %multiply_reduce_fusion.3), channel_id=1, replica_groups=mesh['row'=32,'col'=16] {'row','col'}, use_global_device_ids=true, to_apply=%region_17.0 | all-reduce | flops 16 | bytes 128 | tf_op jit(solution)/shard_map/psum | solution.py:83
  692.5 29.0 %all-gather.2 = f32[32,64,16]{1,2,0:T(8,128)S(1)} all-gather(f32[1,64,16]{1,2,0:T(8,128)S(1)} %bitcast.44), channel_id=1, replica_groups=mesh['row'=32,'col'=16] {'row'}, dimensions={0}, use_global_device_ids=true | all-gather | bytes 135168 | tf_op jit(solution)/shard_map/all_gather | solution.py:91
  721.7 11.9 %while.44 = (s32[]{:T(128)}, f32[16,1024]{1,0:T(8,128)S(1)}, f32[16,2048]{1,0:T(8,128)S(1)}, f32[2048]{0:T(1024)S(1)}, f32[1024]{0:T(1024)S(1)}, /*index=5*/bf16...) while((s32[]{:T(128)}, f32[16,1024]{1,0:T(8,128)S(1)}, ...), condition=%wide.region_20.0_spmd.clone, body=%wide.region_19.0_spmd.clone.sunk | while | flops 173047808 | bytes 4565169 | solution.py:50
  722.3 2.4 fusion.144
  724.7 0.5 fusion.143
  725.3 2.4 fusion.144
  727.7 0.5 fusion.143
  728.2 2.4 fusion.144
  730.7 0.5 fusion.143
  731.2 2.4 fusion.144
  733.6 1.0 copy.36
  734.7 85.5 %reduce-scatter.14.cloned.1.call-done = f32[64,16]{1,0:T(8,128)} async-done(((f32[1024,16]{1,0:T(8,128)}), f32[64,16]{1,0:T(8,128)}) %reduce-scatter.14.cloned.1.call-update) | async-done | bytes 4112
  820.2 1.4 copy.37
  (50 shorter events, 5.0 us)
Async XLA Ops:
  7.2 64.7 %copy-start = (f32[16,64]{1,0:T(8,128)S(1)}, f32[16,64]{1,0:T(8,128)}, u32[]{:S(2)}) copy-start(f32[16,64]{1,0:T(8,128)} %param.15) | copy-start | bytes 12292
  7.2 189.2 %reduce-scatter.10.cloned.1.call-start = ((), (), s32[]{:S(2)}) async-start(), calls=%async_computation.3 | async-start | bytes 557056
  99.6 97.6 %copy-start.2 = (f32[64]{0:T(128)S(1)}, f32[64]{0:T(128)}, u32[]{:S(2)}) copy-start(f32[64]{0:T(128)} %param.14) | copy-start | bytes 772
  112.6 477.0 %reduce-scatter.12.cloned.1.call-start = ((), (), s32[]{:S(2)}) async-start(), calls=%async_computation.4 | async-start | bytes 557056
  505.1 315.0 %reduce-scatter.14.cloned.1.call-start = ((), (), s32[]{:S(2)}) async-start(), calls=%async_computation.5 | async-start | bytes 557056
  692.5 29.2 %copy-start.1 = (f32[16,64]{1,0:T(8,128)}, f32[16,64]{1,0:T(8,128)S(1)}, u32[]{:S(2)}) copy-start(f32[16,64]{1,0:T(8,128)S(1)} %multiply_add_fusion) | copy-start | bytes 12292
Sparse Core Ops, SparseCore 0:
  112.7 83.6 reduce-scatter.9
  505.2 84.2 reduce-scatter.11
  734.8 85.3 reduce-scatter.13
